TPU v7x, 512 devices: a whole 4x4x16 slice. The times are simulated.
512 devices in a mesh: ctx: 16 (over x, z_hi), fsdp: 32 (over z_lo, y, core).
Axes of the slice: x: 4, y: 4, z: 16 (z_hi: 4, z_lo: 4; z = z_hi * 4 + z_lo), core: 2. Of those that a mesh axis runs over, the one named last changes fastest.
Arguments:
- block_pos: int32 [8, 16], P(None, 'ctx'), may hold values from 0 to 15, each once within a row
- queries: bfloat16 [32, 2048, 640], P('fsdp', 'ctx'), may hold values from -6 to 6
- keys: bfloat16 [32, 2048, 128], P('fsdp', 'ctx'), may hold values from -6 to 6
- values: bfloat16 [32, 2048, 128], P('fsdp', 'ctx'), may hold values from -12 to 12
- attention_output: bfloat16 [32, 2048, 640], P('fsdp', 'ctx'), may hold values from -6 to 6
- output_gradient: bfloat16 [32, 2048, 640], P('fsdp', 'ctx'), may hold values from -24 to 24
- log_softmax_norm: float32 [32, 5, 2048], P('fsdp', None, 'ctx'), may hold values from 6 to 9
- features: bfloat16 [8, 2048, 2560], P(None, 'ctx', 'fsdp'), may hold values from -0.119628906 to 0.119628906
Outputs:
- grad_q: bfloat16 [32, 2048, 640], P('fsdp', 'ctx')
- key_gradient: bfloat16 [32, 2048, 128], P('fsdp', 'ctx')
- value_gradient: bfloat16 [32, 2048, 128], P('fsdp', 'ctx')
- grad_wk: float32 [2560, 512], P('fsdp')
Inputs may be any that keep to these rules, and one draw needn't show every extreme that they name: Each row of block_pos holds every block place 0 to 15 once.
All inputs are finite; a program needn't handle non-finite values.
Results may differ from a plain program's by a relative error of at most 0.0058.
Values may be sent and summed in bfloat16 or wider, within the bound.
No kernel may reach another device: no remote copies, remote signals or barrier semaphores. Data moves between devices by JAX's collectives and lax.ppermute only.
A program may use at most 64 MiB of HBM per device.

v0:
```python
import jax
import jax.numpy as jnp
from jax import lax
from jax.sharding import PartitionSpec as P

QUERY_HEADS = 20
KEY_VALUE_HEADS = 4
HEAD_SIZE = 128
HEAD_GROUPS = 4


def from_behind(value, axis, steps):
    count = lax.axis_size(axis)
    pairs = [(source, (source + steps) % count) for source in range(count)]
    return lax.ppermute(value, axis, pairs)


def shortened(shard):

    def short(part):
        return part.astype(jnp.bfloat16) if part.dtype == jnp.float32 else part

    return jax.tree.map(short, shard)


def block_grads(
    heads_of_queries,
    head_gradient,
    delta_heads,
    heads_of_norm,
    block_of_keys,
    block_of_values,
    key_place,
    key_offset,
    own_place,
):
    query_rows = heads_of_queries.shape[0]
    key_rows = block_of_keys.shape[0]
    score_scale = heads_of_queries.shape[-1] ** (-0.5)
    query_pos = own_place * query_rows + lax.iota(jnp.int32, query_rows)
    key_pos = key_place[0] * query_rows + key_offset + lax.iota(jnp.int32, key_rows)
    visible = key_pos[None, :] <= query_pos[:, None]
    scores = (
        jnp.einsum(
            "tkgd,ukd->kgtu", heads_of_queries, block_of_keys, preferred_element_type=jnp.float32
        )
        * score_scale
    )
    soft_probs = jnp.where(visible, jnp.exp(scores - heads_of_norm[..., None]), 0.0)
    dprobs = jnp.einsum(
        "tkgd,ukd->kgtu", head_gradient, block_of_values, preferred_element_type=jnp.float32
    )
    dscores = (soft_probs * (dprobs - delta_heads[..., None]) * score_scale).astype(jnp.bfloat16)
    probs_low = soft_probs.astype(jnp.bfloat16)
    grad_query = jnp.einsum(
        "kgtu,ukd->tkgd", dscores, block_of_keys, preferred_element_type=jnp.float32
    )
    gradient_for_key = jnp.einsum(
        "kgtu,tkgd->ukd", dscores, heads_of_queries, preferred_element_type=jnp.float32
    )
    gradient_for_value = jnp.einsum(
        "kgtu,tkgd->ukd", probs_low, head_gradient, preferred_element_type=jnp.float32
    )
    return (grad_query, gradient_for_key, gradient_for_value)


def local(
    block_pos, queries, keys, values, attention_output, output_gradient, log_softmax_norm, features
):
    rows_per_block = queries.shape[1]
    group_size = QUERY_HEADS // KEY_VALUE_HEADS
    kv_local = keys.shape[-1] // HEAD_SIZE
    sequence_index = lax.axis_index("fsdp") // HEAD_GROUPS
    own_row = lax.dynamic_slice_in_dim(block_pos, sequence_index, 1, 0)
    own_place = own_row[0, 0]
    key_place = own_row[0, 0:1]
    heads_of_queries = queries[0].reshape(rows_per_block, kv_local, group_size, HEAD_SIZE)
    head_gradient = output_gradient[0].reshape(rows_per_block, kv_local, group_size, HEAD_SIZE)
    heads_of_output = attention_output[0].reshape(rows_per_block, kv_local, group_size, HEAD_SIZE)
    delta = jnp.sum(
        head_gradient.astype(jnp.float32) * heads_of_output.astype(jnp.float32), axis=-1
    )
    delta_heads = jnp.transpose(delta, (1, 2, 0))
    heads_of_norm = log_softmax_norm[0].reshape(kv_local, group_size, rows_per_block)
    block_of_keys = keys[0].reshape(rows_per_block, kv_local, HEAD_SIZE)
    block_of_values = values[0].reshape(rows_per_block, kv_local, HEAD_SIZE)
    cycle_length = lax.axis_size("ctx")
    zero_key_gradient = jnp.zeros((rows_per_block, kv_local, HEAD_SIZE), jnp.float32)
    zero_query_gradient = jnp.zeros((rows_per_block, kv_local, group_size, HEAD_SIZE), jnp.float32)

    def visit_rows(query_acc, blocks, grad_pair, key_offset):
        add_query, add_key, add_value = block_grads(
            heads_of_queries,
            head_gradient,
            delta_heads,
            heads_of_norm,
            blocks[0],
            blocks[1],
            blocks[2],
            key_offset,
            own_place,
        )
        return (query_acc + add_query, (grad_pair[0] + add_key, grad_pair[1] + add_value))

    def visit(query_acc, blocks, grad_pair):
        return visit_rows(query_acc, blocks, grad_pair, 0)

    def pass_grads(grad_pair):
        return from_behind(grad_pair, "ctx", 1)

    def cycle_step(step_index, cycle_state):
        query_acc, blocks, grad_pair = cycle_state
        query_acc, grad_pair = visit(query_acc, blocks, grad_pair)
        blocks = jax.tree.map(
            lambda part, own: part.astype(own.dtype),
            from_behind(shortened(blocks), "ctx", 1),
            blocks,
        )
        grad_pair = pass_grads(grad_pair)
        return (query_acc, blocks, grad_pair)

    cycle_state = (
        zero_query_gradient,
        (block_of_keys, block_of_values, key_place),
        (zero_key_gradient, zero_key_gradient),
    )
    query_acc, blocks, grad_pair = lax.fori_loop(0, cycle_length - 1, cycle_step, cycle_state)
    query_acc, grad_pair = visit(query_acc, blocks, grad_pair)
    grad_pair = pass_grads(grad_pair)
    key_gradient_sum = grad_pair[0]
    value_gradient_sum = grad_pair[1]
    grad_q = query_acc.reshape(rows_per_block, -1).astype(jnp.bfloat16)
    key_gradient = key_gradient_sum.reshape(rows_per_block, -1).astype(jnp.bfloat16)
    value_gradient = value_gradient_sum.reshape(rows_per_block, -1).astype(jnp.bfloat16)
    local_width = key_gradient.shape[-1]
    feature_cols = features.shape[-1]
    piece = lax.all_gather(key_gradient[None], "fsdp", axis=0, tiled=True)
    count = piece.shape[0]
    indices = lax.iota(jnp.int32, count)
    seq_ids = indices // HEAD_GROUPS
    group_ids = indices % HEAD_GROUPS
    chosen = jnp.take(features, seq_ids, axis=0)
    contrib = jnp.einsum("pti,ptj->pij", chosen, piece, preferred_element_type=jnp.float32)
    rounded = lax.optimization_barrier(contrib.astype(jnp.bfloat16)).astype(jnp.float32)
    placing = (group_ids[:, None] == lax.iota(jnp.int32, HEAD_GROUPS)[None, :]).astype(jnp.float32)
    summed = jnp.einsum("pij,pr->irj", rounded, placing)
    summed = summed.reshape(feature_cols, HEAD_GROUPS * local_width)
    grad_wk = lax.psum(summed, "ctx")
    return (grad_q[None], key_gradient[None], value_gradient[None], grad_wk)


def solution(mesh):
    return jax.shard_map(
        local,
        mesh=mesh,
        in_specs=(
            P(None, "ctx"),
            P("fsdp", "ctx", None),
            P("fsdp", "ctx", None),
            P("fsdp", "ctx", None),
            P("fsdp", "ctx", None),
            P("fsdp", "ctx", None),
            P("fsdp", None, "ctx"),
            P(None, "ctx", "fsdp"),
        ),
        out_specs=(
            P("fsdp", "ctx", None),
            P("fsdp", "ctx", None),
            P("fsdp", "ctx", None),
            P("fsdp", None),
        ),
        check_vma=False,
    )
```

profile of v0, /device:TPU:2, one launch (start us, length us, event | category | flops | bytes accessed | tf_op | source)
XLA Modules:
  0.0 845.0 jit_solution(10300200507523520744)
XLA Ops:
  12.6 541.2 %while.23 = (s32[]{:T(128)}, f32[128,1,5,128]{3,0,2,1:T(8,128)S(1)}, bf16[128,1,128]{2,0,1:T(8,128)(2,1)S(1)}, bf16[128,1,128]{2,0,1:T(8,128)(2,1)S(1)}, s32[1]{...) while((s32[]{:T(128)}, ...), condition=%wide.region_2.3_spmd.clone, body=%wide.region_1.2_spmd.clone.sunk | while | flops 105726208 | bytes 4103563 | solution.py:127
  12.6 9.1 %collective-permute-start = (bf16[128,1,128]{2,0,1:T(8,128)(2,1)S(1)}, bf16[128,1,128]{2,0,1:T(8,128)(2,1)S(1)}, u32[]{:S(2)}, u32[]{:S(2)}) collective-permute-start(bf16[128,1,128]{2,0,1:T(8,128)(2,1)S(1)} %copy.66), channel_id=1, source_target_pairs={{0,32},{32,64},{64,96},{96,128},{128,160},{160,192},{192,224},{224... | collective-permute-start | bytes 98312 | tf_op jit(solution)/shard_map/while/body/eval_jaxpr/ppermute | solution.py:15
  21.7 9.1 %collective-permute-start.1 = (bf16[128,1,128]{2,0,1:T(8,128)(2,1)S(1)}, bf16[128,1,128]{2,0,1:T(8,128)(2,1)S(1)}, u32[]{:S(2)}, u32[]{:S(2)}) collective-permute-start(bf16[128,1,128]{2,0,1:T(8,128)(2,1)S(1)} %copy.67), channel_id=1, source_target_pairs={{0,32},{32,64},{64,96},{96,128},{128,160},{160,192},{192,224},{224... | collective-permute-start | bytes 98312 | tf_op jit(solution)/shard_map/while/body/eval_jaxpr/ppermute | solution.py:15
  31.4 5.6 collective-permute-start.2
  45.9 7.4 collective-permute-done.3
  57.8 8.3 collective-permute-start.1
  94.6 8.3 collective-permute-start.1
  119.1 6.7 collective-permute-done.4
  125.8 8.3 collective-permute-start
  148.5 7.0 collective-permute-start.4
  160.6 6.0 collective-permute-start
  166.6 6.5 collective-permute-start.1
  180.2 6.9 collective-permute-start.3
  192.3 5.9 collective-permute-done.4
  201.6 6.5 collective-permute-start.1
  208.6 7.9 collective-permute-start.2
  236.2 6.1 collective-permute-start.1
  247.4 7.0 collective-permute-start.3
  254.6 8.1 collective-permute-start.4
  266.0 6.8 collective-permute-start
  272.8 5.9 collective-permute-start.1
  284.9 6.5 collective-permute-start.3
  291.6 5.5 collective-permute-start.4
  297.5 7.8 collective-permute-done.4
  308.2 8.9 %collective-permute-start.1 = (bf16[128,1,128]{2,0,1:T(8,128)(2,1)S(1)}, bf16[128,1,128]{2,0,1:T(8,128)(2,1)S(1)}, u32[]{:S(2)}, u32[]{:S(2)}) collective-permute-start(bf16[128,1,128]{2,0,1:T(8,128)(2,1)S(1)} %copy.67), channel_id=1, source_target_pairs={{0,32},{32,64},{64,96},{96,128},{128,160},{160,192},{192,224},{224... | collective-permute-start | bytes 98312 | tf_op jit(solution)/shard_map/while/body/eval_jaxpr/ppermute | solution.py:15
  322.3 6.0 collective-permute-start.3
  333.6 6.4 collective-permute-done.4
  341.9 7.4 collective-permute-start.1
  349.8 9.7 %collective-permute-start.2 = (s32[1]{0:T(128)}, s32[1]{0:T(128)}, u32[]{:S(2)}, u32[]{:S(2)}) collective-permute-start(s32[1]{0:T(128)} %copy.68), channel_id=1, source_target_pairs={{0,32},{32,64},{64,96},{96,128},{128,160},{160,192},{192,224},{224... | collective-permute-start | bytes 20 | tf_op jit(solution)/shard_map/while/body/eval_jaxpr/ppermute | solution.py:15
  367.1 6.4 collective-permute-done.3
  384.5 7.4 collective-permute-start.2
  398.7 6.0 collective-permute-start.4
  405.2 5.6 collective-permute-done.4
  415.0 7.3 collective-permute-start.1
  422.8 6.1 collective-permute-start.2
  435.3 6.0 collective-permute-start.4
  446.3 6.5 collective-permute-start
  452.8 6.1 collective-permute-start.1
  465.1 5.7 collective-permute-start.3
  476.0 6.7 collective-permute-done.4
  490.0 9.6 %collective-permute-start.2 = (s32[1]{0:T(128)}, s32[1]{0:T(128)}, u32[]{:S(2)}, u32[]{:S(2)}) collective-permute-start(s32[1]{0:T(128)} %copy.68), channel_id=1, source_target_pairs={{0,32},{32,64},{64,96},{96,128},{128,160},{160,192},{192,224},{224... | collective-permute-start | bytes 20 | tf_op jit(solution)/shard_map/while/body/eval_jaxpr/ppermute | solution.py:15
  512.0 6.8 collective-permute-done.4
  523.2 8.2 collective-permute-start.2
  532.8 9.4 %collective-permute-start.3 = (f32[128,1,128]{2,0,1:T(8,128)S(1)}, f32[128,1,128]{2,0,1:T(8,128)S(1)}, u32[]{:S(2)}, u32[]{:S(2)}) collective-permute-start(f32[128,1,128]{2,0,1:T(8,128)S(1)} %fusion.89), channel_id=1, source_target_pairs={{0,32},{32,64},{64,96},{96,128},{128,160},{160,192},{192,224},{224... | collective-permute-start | bytes 196616 | tf_op jit(solution)/shard_map/while/body/eval_jaxpr/ppermute | solution.py:15
  544.7 9.1 %collective-permute-done.4 = f32[128,1,128]{2,0,1:T(8,128)S(1)} collective-permute-done((f32[128,1,128]{2,0,1:T(8,128)S(1)}, f32[128,1,128]{2,0,1:T(8,128)S(1)}, u32[]{:S(2)}, u32[]{:S(2)}) %collective-permute-start.4) | collective-permute-done | bytes 65568 | tf_op jit(solution)/shard_map/while/body/eval_jaxpr/ppermute | solution.py:15
  557.7 8.7 %collective-permute-done.5 = bf16[128,1,128]{2,0,1:T(8,128)(2,1)S(1)} collective-permute-done((bf16[128,1,128]{2,0,1:T(8,128)(2,1)S(1)}, bf16[128,1,128]{2,0,1:T(8,128)(2,1)S(1)}, u32[]{:S(2)}, u32[]{:S(2)}) %collective-permute-start.5) | collective-permute-done | bytes 32800 | tf_op jit(solution)/shard_map/ppermute | solution.py:15
  570.1 63.8 %all-gather.3.cloned.1.call-done = bf16[4096,1,128]{2,0,1:T(8,128)(2,1)} async-done(((bf16[128,1,128]{2,0,1:T(8,128)(2,1)}), bf16[4096,1,128]{2,0,1:T(8,128)(2,1)}) %all-gather.3.cloned.1.call-update) | async-done | bytes 1048592 | tf_op jit(solution)/shard_map/all_gather | solution.py:137
  637.8 197.5 %all-reduce.2.cloned.1.call-done = f32[80,512]{1,0:T(8,128)} async-done(((f32[80,512]{1,0:T(8,128)}), f32[80,512]{1,0:T(8,128)}) %all-reduce.2.cloned.1.call-update) | async-done | bytes 163856 | tf_op jit(solution)/shard_map/psum | solution.py:148
  (315 shorter events, 235.7 us)
Async XLA Ops:
  7.2 626.7 %all-gather.3.cloned.1.call-start = ((), (), s32[]{:S(2)}) async-start(), calls=%async_computation.1 | async-start | bytes 1081344 | tf_op jit(solution)/shard_map/all_gather | solution.py:137
  12.6 33.3 %collective-permute-start = (bf16[128,1,128]{2,0,1:T(8,128)(2,1)S(1)}, bf16[128,1,128]{2,0,1:T(8,128)(2,1)S(1)}, u32[]{:S(2)}, u32[]{:S(2)}) collective-permute-start(bf16[128,1,128]{2,0,1:T(8,128)(2,1)S(1)} %copy.66), channel_id=1, source_target_pairs={{0,32},{32,64},{64,96},{96,128},{128,160},{160,192},{192,224},{224... | collective-permute-start | bytes 98312 | tf_op jit(solution)/shard_map/while/body/eval_jaxpr/ppermute | solution.py:15
  21.7 24.2 %collective-permute-start.1 = (bf16[128,1,128]{2,0,1:T(8,128)(2,1)S(1)}, bf16[128,1,128]{2,0,1:T(8,128)(2,1)S(1)}, u32[]{:S(2)}, u32[]{:S(2)}) collective-permute-start(bf16[128,1,128]{2,0,1:T(8,128)(2,1)S(1)} %copy.67), channel_id=1, source_target_pairs={{0,32},{32,64},{64,96},{96,128},{128,160},{160,192},{192,224},{224... | collective-permute-start | bytes 98312 | tf_op jit(solution)/shard_map/while/body/eval_jaxpr/ppermute | solution.py:15
  31.4 14.5 %collective-permute-start.2 = (s32[1]{0:T(128)}, s32[1]{0:T(128)}, u32[]{:S(2)}, u32[]{:S(2)}) collective-permute-start(s32[1]{0:T(128)} %copy.68), channel_id=1, source_target_pairs={{0,32},{32,64},{64,96},{96,128},{128,160},{160,192},{192,224},{224... | collective-permute-start | bytes 20 | tf_op jit(solution)/shard_map/while/body/eval_jaxpr/ppermute | solution.py:15
  38.3 15.0 %collective-permute-start.3 = (f32[128,1,128]{2,0,1:T(8,128)S(1)}, f32[128,1,128]{2,0,1:T(8,128)S(1)}, u32[]{:S(2)}, u32[]{:S(2)}) collective-permute-start(f32[128,1,128]{2,0,1:T(8,128)S(1)} %fusion.89), channel_id=1, source_target_pairs={{0,32},{32,64},{64,96},{96,128},{128,160},{160,192},{192,224},{224... | collective-permute-start | bytes 196616 | tf_op jit(solution)/shard_map/while/body/eval_jaxpr/ppermute | solution.py:15
  54.0 27.8 %collective-permute-start = (bf16[128,1,128]{2,0,1:T(8,128)(2,1)S(1)}, bf16[128,1,128]{2,0,1:T(8,128)(2,1)S(1)}, u32[]{:S(2)}, u32[]{:S(2)}) collective-permute-start(bf16[128,1,128]{2,0,1:T(8,128)(2,1)S(1)} %copy.66), channel_id=1, source_target_pairs={{0,32},{32,64},{64,96},{96,128},{128,160},{160,192},{192,224},{224... | collective-permute-start | bytes 98312 | tf_op jit(solution)/shard_map/while/body/eval_jaxpr/ppermute | solution.py:15
  57.8 24.0 %collective-permute-start.1 = (bf16[128,1,128]{2,0,1:T(8,128)(2,1)S(1)}, bf16[128,1,128]{2,0,1:T(8,128)(2,1)S(1)}, u32[]{:S(2)}, u32[]{:S(2)}) collective-permute-start(bf16[128,1,128]{2,0,1:T(8,128)(2,1)S(1)} %copy.67), channel_id=1, source_target_pairs={{0,32},{32,64},{64,96},{96,128},{128,160},{160,192},{192,224},{224... | collective-permute-start | bytes 98312 | tf_op jit(solution)/shard_map/while/body/eval_jaxpr/ppermute | solution.py:15
  66.7 15.1 %collective-permute-start.2 = (s32[1]{0:T(128)}, s32[1]{0:T(128)}, u32[]{:S(2)}, u32[]{:S(2)}) collective-permute-start(s32[1]{0:T(128)} %copy.68), channel_id=1, source_target_pairs={{0,32},{32,64},{64,96},{96,128},{128,160},{160,192},{192,224},{224... | collective-permute-start | bytes 20 | tf_op jit(solution)/shard_map/while/body/eval_jaxpr/ppermute | solution.py:15
  89.6 28.9 %collective-permute-start = (bf16[128,1,128]{2,0,1:T(8,128)(2,1)S(1)}, bf16[128,1,128]{2,0,1:T(8,128)(2,1)S(1)}, u32[]{:S(2)}, u32[]{:S(2)}) collective-permute-start(bf16[128,1,128]{2,0,1:T(8,128)(2,1)S(1)} %copy.66), channel_id=1, source_target_pairs={{0,32},{32,64},{64,96},{96,128},{128,160},{160,192},{192,224},{224... | collective-permute-start | bytes 98312 | tf_op jit(solution)/shard_map/while/body/eval_jaxpr/ppermute | solution.py:15
  94.6 23.9 %collective-permute-start.1 = (bf16[128,1,128]{2,0,1:T(8,128)(2,1)S(1)}, bf16[128,1,128]{2,0,1:T(8,128)(2,1)S(1)}, u32[]{:S(2)}, u32[]{:S(2)}) collective-permute-start(bf16[128,1,128]{2,0,1:T(8,128)(2,1)S(1)} %copy.67), channel_id=1, source_target_pairs={{0,32},{32,64},{64,96},{96,128},{128,160},{160,192},{192,224},{224... | collective-permute-start | bytes 98312 | tf_op jit(solution)/shard_map/while/body/eval_jaxpr/ppermute | solution.py:15
  103.5 15.0 %collective-permute-start.2 = (s32[1]{0:T(128)}, s32[1]{0:T(128)}, u32[]{:S(2)}, u32[]{:S(2)}) collective-permute-start(s32[1]{0:T(128)} %copy.68), channel_id=1, source_target_pairs={{0,32},{32,64},{64,96},{96,128},{128,160},{160,192},{192,224},{224... | collective-permute-start | bytes 20 | tf_op jit(solution)/shard_map/while/body/eval_jaxpr/ppermute | solution.py:15
  125.8 30.1 %collective-permute-start = (bf16[128,1,128]{2,0,1:T(8,128)(2,1)S(1)}, bf16[128,1,128]{2,0,1:T(8,128)(2,1)S(1)}, u32[]{:S(2)}, u32[]{:S(2)}) collective-permute-start(bf16[128,1,128]{2,0,1:T(8,128)(2,1)S(1)} %copy.66), channel_id=1, source_target_pairs={{0,32},{32,64},{64,96},{96,128},{128,160},{160,192},{192,224},{224... | collective-permute-start | bytes 98312 | tf_op jit(solution)/shard_map/while/body/eval_jaxpr/ppermute | solution.py:15
  134.1 21.8 %collective-permute-start.1 = (bf16[128,1,128]{2,0,1:T(8,128)(2,1)S(1)}, bf16[128,1,128]{2,0,1:T(8,128)(2,1)S(1)}, u32[]{:S(2)}, u32[]{:S(2)}) collective-permute-start(bf16[128,1,128]{2,0,1:T(8,128)(2,1)S(1)} %copy.67), channel_id=1, source_target_pairs={{0,32},{32,64},{64,96},{96,128},{128,160},{160,192},{192,224},{224... | collective-permute-start | bytes 98312 | tf_op jit(solution)/shard_map/while/body/eval_jaxpr/ppermute | solution.py:15
  138.2 17.6 %collective-permute-start.2 = (s32[1]{0:T(128)}, s32[1]{0:T(128)}, u32[]{:S(2)}, u32[]{:S(2)}) collective-permute-start(s32[1]{0:T(128)} %copy.68), channel_id=1, source_target_pairs={{0,32},{32,64},{64,96},{96,128},{128,160},{160,192},{192,224},{224... | collective-permute-start | bytes 20 | tf_op jit(solution)/shard_map/while/body/eval_jaxpr/ppermute | solution.py:15
  160.6 30.4 %collective-permute-start = (bf16[128,1,128]{2,0,1:T(8,128)(2,1)S(1)}, bf16[128,1,128]{2,0,1:T(8,128)(2,1)S(1)}, u32[]{:S(2)}, u32[]{:S(2)}) collective-permute-start(bf16[128,1,128]{2,0,1:T(8,128)(2,1)S(1)} %copy.66), channel_id=1, source_target_pairs={{0,32},{32,64},{64,96},{96,128},{128,160},{160,192},{192,224},{224... | collective-permute-start | bytes 98312 | tf_op jit(solution)/shard_map/while/body/eval_jaxpr/ppermute | solution.py:15
  166.6 24.4 %collective-permute-start.1 = (bf16[128,1,128]{2,0,1:T(8,128)(2,1)S(1)}, bf16[128,1,128]{2,0,1:T(8,128)(2,1)S(1)}, u32[]{:S(2)}, u32[]{:S(2)}) collective-permute-start(bf16[128,1,128]{2,0,1:T(8,128)(2,1)S(1)} %copy.67), channel_id=1, source_target_pairs={{0,32},{32,64},{64,96},{96,128},{128,160},{160,192},{192,224},{224... | collective-permute-start | bytes 98312 | tf_op jit(solution)/shard_map/while/body/eval_jaxpr/ppermute | solution.py:15
  173.7 17.4 %collective-permute-start.2 = (s32[1]{0:T(128)}, s32[1]{0:T(128)}, u32[]{:S(2)}, u32[]{:S(2)}) collective-permute-start(s32[1]{0:T(128)} %copy.68), channel_id=1, source_target_pairs={{0,32},{32,64},{64,96},{96,128},{128,160},{160,192},{192,224},{224... | collective-permute-start | bytes 20 | tf_op jit(solution)/shard_map/while/body/eval_jaxpr/ppermute | solution.py:15
  198.3 27.4 %collective-permute-start = (bf16[128,1,128]{2,0,1:T(8,128)(2,1)S(1)}, bf16[128,1,128]{2,0,1:T(8,128)(2,1)S(1)}, u32[]{:S(2)}, u32[]{:S(2)}) collective-permute-start(bf16[128,1,128]{2,0,1:T(8,128)(2,1)S(1)} %copy.66), channel_id=1, source_target_pairs={{0,32},{32,64},{64,96},{96,128},{128,160},{160,192},{192,224},{224... | collective-permute-start | bytes 98312 | tf_op jit(solution)/shard_map/while/body/eval_jaxpr/ppermute | solution.py:15
  201.6 24.1 %collective-permute-start.1 = (bf16[128,1,128]{2,0,1:T(8,128)(2,1)S(1)}, bf16[128,1,128]{2,0,1:T(8,128)(2,1)S(1)}, u32[]{:S(2)}, u32[]{:S(2)}) collective-permute-start(bf16[128,1,128]{2,0,1:T(8,128)(2,1)S(1)} %copy.67), channel_id=1, source_target_pairs={{0,32},{32,64},{64,96},{96,128},{128,160},{160,192},{192,224},{224... | collective-permute-start | bytes 98312 | tf_op jit(solution)/shard_map/while/body/eval_jaxpr/ppermute | solution.py:15
  208.6 17.0 %collective-permute-start.2 = (s32[1]{0:T(128)}, s32[1]{0:T(128)}, u32[]{:S(2)}, u32[]{:S(2)}) collective-permute-start(s32[1]{0:T(128)} %copy.68), channel_id=1, source_target_pairs={{0,32},{32,64},{64,96},{96,128},{128,160},{160,192},{192,224},{224... | collective-permute-start | bytes 20 | tf_op jit(solution)/shard_map/while/body/eval_jaxpr/ppermute | solution.py:15
  233.6 29.4 %collective-permute-start = (bf16[128,1,128]{2,0,1:T(8,128)(2,1)S(1)}, bf16[128,1,128]{2,0,1:T(8,128)(2,1)S(1)}, u32[]{:S(2)}, u32[]{:S(2)}) collective-permute-start(bf16[128,1,128]{2,0,1:T(8,128)(2,1)S(1)} %copy.66), channel_id=1, source_target_pairs={{0,32},{32,64},{64,96},{96,128},{128,160},{160,192},{192,224},{224... | collective-permute-start | bytes 98312 | tf_op jit(solution)/shard_map/while/body/eval_jaxpr/ppermute | solution.py:15
  236.2 26.9 %collective-permute-start.1 = (bf16[128,1,128]{2,0,1:T(8,128)(2,1)S(1)}, bf16[128,1,128]{2,0,1:T(8,128)(2,1)S(1)}, u32[]{:S(2)}, u32[]{:S(2)}) collective-permute-start(bf16[128,1,128]{2,0,1:T(8,128)(2,1)S(1)} %copy.67), channel_id=1, source_target_pairs={{0,32},{32,64},{64,96},{96,128},{128,160},{160,192},{192,224},{224... | collective-permute-start | bytes 98312 | tf_op jit(solution)/shard_map/while/body/eval_jaxpr/ppermute | solution.py:15
  242.8 20.2 %collective-permute-start.2 = (s32[1]{0:T(128)}, s32[1]{0:T(128)}, u32[]{:S(2)}, u32[]{:S(2)}) collective-permute-start(s32[1]{0:T(128)} %copy.68), channel_id=1, source_target_pairs={{0,32},{32,64},{64,96},{96,128},{128,160},{160,192},{192,224},{224... | collective-permute-start | bytes 20 | tf_op jit(solution)/shard_map/while/body/eval_jaxpr/ppermute | solution.py:15
  247.4 15.6 %collective-permute-start.3 = (f32[128,1,128]{2,0,1:T(8,128)S(1)}, f32[128,1,128]{2,0,1:T(8,128)S(1)}, u32[]{:S(2)}, u32[]{:S(2)}) collective-permute-start(f32[128,1,128]{2,0,1:T(8,128)S(1)} %fusion.89), channel_id=1, source_target_pairs={{0,32},{32,64},{64,96},{96,128},{128,160},{160,192},{192,224},{224... | collective-permute-start | bytes 196616 | tf_op jit(solution)/shard_map/while/body/eval_jaxpr/ppermute | solution.py:15
  266.0 31.5 %collective-permute-start = (bf16[128,1,128]{2,0,1:T(8,128)(2,1)S(1)}, bf16[128,1,128]{2,0,1:T(8,128)(2,1)S(1)}, u32[]{:S(2)}, u32[]{:S(2)}) collective-permute-start(bf16[128,1,128]{2,0,1:T(8,128)(2,1)S(1)} %copy.66), channel_id=1, source_target_pairs={{0,32},{32,64},{64,96},{96,128},{128,160},{160,192},{192,224},{224... | collective-permute-start | bytes 98312 | tf_op jit(solution)/shard_map/while/body/eval_jaxpr/ppermute | solution.py:15
  272.8 24.7 %collective-permute-start.1 = (bf16[128,1,128]{2,0,1:T(8,128)(2,1)S(1)}, bf16[128,1,128]{2,0,1:T(8,128)(2,1)S(1)}, u32[]{:S(2)}, u32[]{:S(2)}) collective-permute-start(bf16[128,1,128]{2,0,1:T(8,128)(2,1)S(1)} %copy.67), channel_id=1, source_target_pairs={{0,32},{32,64},{64,96},{96,128},{128,160},{160,192},{192,224},{224... | collective-permute-start | bytes 98312 | tf_op jit(solution)/shard_map/while/body/eval_jaxpr/ppermute | solution.py:15
  279.3 18.2 %collective-permute-start.2 = (s32[1]{0:T(128)}, s32[1]{0:T(128)}, u32[]{:S(2)}, u32[]{:S(2)}) collective-permute-start(s32[1]{0:T(128)} %copy.68), channel_id=1, source_target_pairs={{0,32},{32,64},{64,96},{96,128},{128,160},{160,192},{192,224},{224... | collective-permute-start | bytes 20 | tf_op jit(solution)/shard_map/while/body/eval_jaxpr/ppermute | solution.py:15
  305.3 25.5 %collective-permute-start = (bf16[128,1,128]{2,0,1:T(8,128)(2,1)S(1)}, bf16[128,1,128]{2,0,1:T(8,128)(2,1)S(1)}, u32[]{:S(2)}, u32[]{:S(2)}) collective-permute-start(bf16[128,1,128]{2,0,1:T(8,128)(2,1)S(1)} %copy.66), channel_id=1, source_target_pairs={{0,32},{32,64},{64,96},{96,128},{128,160},{160,192},{192,224},{224... | collective-permute-start | bytes 98312 | tf_op jit(solution)/shard_map/while/body/eval_jaxpr/ppermute | solution.py:15
  308.2 22.6 %collective-permute-start.1 = (bf16[128,1,128]{2,0,1:T(8,128)(2,1)S(1)}, bf16[128,1,128]{2,0,1:T(8,128)(2,1)S(1)}, u32[]{:S(2)}, u32[]{:S(2)}) collective-permute-start(bf16[128,1,128]{2,0,1:T(8,128)(2,1)S(1)} %copy.67), channel_id=1, source_target_pairs={{0,32},{32,64},{64,96},{96,128},{128,160},{160,192},{192,224},{224... | collective-permute-start | bytes 98312 | tf_op jit(solution)/shard_map/while/body/eval_jaxpr/ppermute | solution.py:15
  340.0 27.1 %collective-permute-start = (bf16[128,1,128]{2,0,1:T(8,128)(2,1)S(1)}, bf16[128,1,128]{2,0,1:T(8,128)(2,1)S(1)}, u32[]{:S(2)}, u32[]{:S(2)}) collective-permute-start(bf16[128,1,128]{2,0,1:T(8,128)(2,1)S(1)} %copy.66), channel_id=1, source_target_pairs={{0,32},{32,64},{64,96},{96,128},{128,160},{160,192},{192,224},{224... | collective-permute-start | bytes 98312 | tf_op jit(solution)/shard_map/while/body/eval_jaxpr/ppermute | solution.py:15
  341.9 25.1 %collective-permute-start.1 = (bf16[128,1,128]{2,0,1:T(8,128)(2,1)S(1)}, bf16[128,1,128]{2,0,1:T(8,128)(2,1)S(1)}, u32[]{:S(2)}, u32[]{:S(2)}) collective-permute-start(bf16[128,1,128]{2,0,1:T(8,128)(2,1)S(1)} %copy.67), channel_id=1, source_target_pairs={{0,32},{32,64},{64,96},{96,128},{128,160},{160,192},{192,224},{224... | collective-permute-start | bytes 98312 | tf_op jit(solution)/shard_map/while/body/eval_jaxpr/ppermute | solution.py:15
  349.8 17.2 %collective-permute-start.2 = (s32[1]{0:T(128)}, s32[1]{0:T(128)}, u32[]{:S(2)}, u32[]{:S(2)}) collective-permute-start(s32[1]{0:T(128)} %copy.68), channel_id=1, source_target_pairs={{0,32},{32,64},{64,96},{96,128},{128,160},{160,192},{192,224},{224... | collective-permute-start | bytes 20 | tf_op jit(solution)/shard_map/while/body/eval_jaxpr/ppermute | solution.py:15
  375.7 29.3 %collective-permute-start = (bf16[128,1,128]{2,0,1:T(8,128)(2,1)S(1)}, bf16[128,1,128]{2,0,1:T(8,128)(2,1)S(1)}, u32[]{:S(2)}, u32[]{:S(2)}) collective-permute-start(bf16[128,1,128]{2,0,1:T(8,128)(2,1)S(1)} %copy.66), channel_id=1, source_target_pairs={{0,32},{32,64},{64,96},{96,128},{128,160},{160,192},{192,224},{224... | collective-permute-start | bytes 98312 | tf_op jit(solution)/shard_map/while/body/eval_jaxpr/ppermute | solution.py:15
  378.6 26.4 %collective-permute-start.1 = (bf16[128,1,128]{2,0,1:T(8,128)(2,1)S(1)}, bf16[128,1,128]{2,0,1:T(8,128)(2,1)S(1)}, u32[]{:S(2)}, u32[]{:S(2)}) collective-permute-start(bf16[128,1,128]{2,0,1:T(8,128)(2,1)S(1)} %copy.67), channel_id=1, source_target_pairs={{0,32},{32,64},{64,96},{96,128},{128,160},{160,192},{192,224},{224... | collective-permute-start | bytes 98312 | tf_op jit(solution)/shard_map/while/body/eval_jaxpr/ppermute | solution.py:15
  384.5 20.5 %collective-permute-start.2 = (s32[1]{0:T(128)}, s32[1]{0:T(128)}, u32[]{:S(2)}, u32[]{:S(2)}) collective-permute-start(s32[1]{0:T(128)} %copy.68), channel_id=1, source_target_pairs={{0,32},{32,64},{64,96},{96,128},{128,160},{160,192},{192,224},{224... | collective-permute-start | bytes 20 | tf_op jit(solution)/shard_map/while/body/eval_jaxpr/ppermute | solution.py:15
  410.8 30.8 %collective-permute-start = (bf16[128,1,128]{2,0,1:T(8,128)(2,1)S(1)}, bf16[128,1,128]{2,0,1:T(8,128)(2,1)S(1)}, u32[]{:S(2)}, u32[]{:S(2)}) collective-permute-start(bf16[128,1,128]{2,0,1:T(8,128)(2,1)S(1)} %copy.66), channel_id=1, source_target_pairs={{0,32},{32,64},{64,96},{96,128},{128,160},{160,192},{192,224},{224... | collective-permute-start | bytes 98312 | tf_op jit(solution)/shard_map/while/body/eval_jaxpr/ppermute | solution.py:15
  415.0 26.7 %collective-permute-start.1 = (bf16[128,1,128]{2,0,1:T(8,128)(2,1)S(1)}, bf16[128,1,128]{2,0,1:T(8,128)(2,1)S(1)}, u32[]{:S(2)}, u32[]{:S(2)}) collective-permute-start(bf16[128,1,128]{2,0,1:T(8,128)(2,1)S(1)} %copy.67), channel_id=1, source_target_pairs={{0,32},{32,64},{64,96},{96,128},{128,160},{160,192},{192,224},{224... | collective-permute-start | bytes 98312 | tf_op jit(solution)/shard_map/while/body/eval_jaxpr/ppermute | solution.py:15
  422.8 18.8 %collective-permute-start.2 = (s32[1]{0:T(128)}, s32[1]{0:T(128)}, u32[]{:S(2)}, u32[]{:S(2)}) collective-permute-start(s32[1]{0:T(128)} %copy.68), channel_id=1, source_target_pairs={{0,32},{32,64},{64,96},{96,128},{128,160},{160,192},{192,224},{224... | collective-permute-start | bytes 20 | tf_op jit(solution)/shard_map/while/body/eval_jaxpr/ppermute | solution.py:15
  446.3 26.8 %collective-permute-start = (bf16[128,1,128]{2,0,1:T(8,128)(2,1)S(1)}, bf16[128,1,128]{2,0,1:T(8,128)(2,1)S(1)}, u32[]{:S(2)}, u32[]{:S(2)}) collective-permute-start(bf16[128,1,128]{2,0,1:T(8,128)(2,1)S(1)} %copy.66), channel_id=1, source_target_pairs={{0,32},{32,64},{64,96},{96,128},{128,160},{160,192},{192,224},{224... | collective-permute-start | bytes 98312 | tf_op jit(solution)/shard_map/while/body/eval_jaxpr/ppermute | solution.py:15
  452.8 20.3 %collective-permute-start.1 = (bf16[128,1,128]{2,0,1:T(8,128)(2,1)S(1)}, bf16[128,1,128]{2,0,1:T(8,128)(2,1)S(1)}, u32[]{:S(2)}, u32[]{:S(2)}) collective-permute-start(bf16[128,1,128]{2,0,1:T(8,128)(2,1)S(1)} %copy.67), channel_id=1, source_target_pairs={{0,32},{32,64},{64,96},{96,128},{128,160},{160,192},{192,224},{224... | collective-permute-start | bytes 98312 | tf_op jit(solution)/shard_map/while/body/eval_jaxpr/ppermute | solution.py:15
  482.7 25.7 %collective-permute-start = (bf16[128,1,128]{2,0,1:T(8,128)(2,1)S(1)}, bf16[128,1,128]{2,0,1:T(8,128)(2,1)S(1)}, u32[]{:S(2)}, u32[]{:S(2)}) collective-permute-start(bf16[128,1,128]{2,0,1:T(8,128)(2,1)S(1)} %copy.66), channel_id=1, source_target_pairs={{0,32},{32,64},{64,96},{96,128},{128,160},{160,192},{192,224},{224... | collective-permute-start | bytes 98312 | tf_op jit(solution)/shard_map/while/body/eval_jaxpr/ppermute | solution.py:15
  484.6 23.8 %collective-permute-start.1 = (bf16[128,1,128]{2,0,1:T(8,128)(2,1)S(1)}, bf16[128,1,128]{2,0,1:T(8,128)(2,1)S(1)}, u32[]{:S(2)}, u32[]{:S(2)}) collective-permute-start(bf16[128,1,128]{2,0,1:T(8,128)(2,1)S(1)} %copy.67), channel_id=1, source_target_pairs={{0,32},{32,64},{64,96},{96,128},{128,160},{160,192},{192,224},{224... | collective-permute-start | bytes 98312 | tf_op jit(solution)/shard_map/while/body/eval_jaxpr/ppermute | solution.py:15
  490.0 18.4 %collective-permute-start.2 = (s32[1]{0:T(128)}, s32[1]{0:T(128)}, u32[]{:S(2)}, u32[]{:S(2)}) collective-permute-start(s32[1]{0:T(128)} %copy.68), channel_id=1, source_target_pairs={{0,32},{32,64},{64,96},{96,128},{128,160},{160,192},{192,224},{224... | collective-permute-start | bytes 20 | tf_op jit(solution)/shard_map/while/body/eval_jaxpr/ppermute | solution.py:15
  518.8 25.9 %collective-permute-start = (bf16[128,1,128]{2,0,1:T(8,128)(2,1)S(1)}, bf16[128,1,128]{2,0,1:T(8,128)(2,1)S(1)}, u32[]{:S(2)}, u32[]{:S(2)}) collective-permute-start(bf16[128,1,128]{2,0,1:T(8,128)(2,1)S(1)} %copy.66), channel_id=1, source_target_pairs={{0,32},{32,64},{64,96},{96,128},{128,160},{160,192},{192,224},{224... | collective-permute-start | bytes 98312 | tf_op jit(solution)/shard_map/while/body/eval_jaxpr/ppermute | solution.py:15
  520.7 24.0 %collective-permute-start.1 = (bf16[128,1,128]{2,0,1:T(8,128)(2,1)S(1)}, bf16[128,1,128]{2,0,1:T(8,128)(2,1)S(1)}, u32[]{:S(2)}, u32[]{:S(2)}) collective-permute-start(bf16[128,1,128]{2,0,1:T(8,128)(2,1)S(1)} %copy.67), channel_id=1, source_target_pairs={{0,32},{32,64},{64,96},{96,128},{128,160},{160,192},{192,224},{224... | collective-permute-start | bytes 98312 | tf_op jit(solution)/shard_map/while/body/eval_jaxpr/ppermute | solution.py:15
  523.2 21.5 %collective-permute-start.2 = (s32[1]{0:T(128)}, s32[1]{0:T(128)}, u32[]{:S(2)}, u32[]{:S(2)}) collective-permute-start(s32[1]{0:T(128)} %copy.68), channel_id=1, source_target_pairs={{0,32},{32,64},{64,96},{96,128},{128,160},{160,192},{192,224},{224... | collective-permute-start | bytes 20 | tf_op jit(solution)/shard_map/while/body/eval_jaxpr/ppermute | solution.py:15
  567.0 268.3 %all-reduce.2.cloned.1.call-start = ((), (), s32[]{:S(2)}) async-start(), calls=%async_computation | async-start | bytes 327680 | tf_op jit(solution)/shard_map/psum | solution.py:148
  567.3 70.6 %collective-permute-start.6 = (bf16[128,1,128]{2,0,1:T(8,128)(2,1)S(1)}, bf16[128,1,128]{2,0,1:T(8,128)(2,1)S(1)}, u32[]{:S(2)}, u32[]{:S(2)}) collective-permute-start(bf16[128,1,128]{2,0,1:T(8,128)(2,1)S(1)} %fusion.33), channel_id=1, source_target_pairs={{0,32},{32,64},{64,96},{96,128},{128,160},{160,192},{192,224},{224... | collective-permute-start | bytes 98312 | tf_op jit(solution)/shard_map/ppermute | solution.py:15
  (41 other events, 1141.5 us)
Sparse Core Ops, SparseCore 0:
  567.1 66.7 all-gather.2
  637.4 197.8 all-reduce.1
where the time goes:
time: 848 us; the launch traced here: 845 us
  starting transfers between devices  396 us (47%)
  waiting for transfers between devices  381 us (45%)
  matrix products  19.6 us (2%)
  between operations  14.8 us (2%)
  other arithmetic  12.4 us (1%)
  local copies, waits for them, and re-layouts  10.7 us (1%)
  loops' own time  10.2 us (1%)
    ppermute x77, starting transfers between devices, from_behind(): return lax.ppermute(value, axis, pairs)  396 us
    psum x1, waiting for transfers between devices, local(): grad_wk = lax.psum(summed, 'ctx')  197 us
    ppermute x77, waiting for transfers between devices, from_behind(): return lax.ppermute(value, axis, pairs)  120 us
    all_gather x1, waiting for transfers between devices, local(): piece = lax.all_gather(key_gradient[None], 'fsdp', axis=0, tiled=True)  63.8 us
  transfers between devices with their start and end apart: 79, of which 30 were waited for; matrix products, arithmetic and copies ran while one was open for 4% of the time, Pallas kernels for 0%

commit v1 on v0

--- a/solution.py
+++ b/solution.py
@@ -134,7 +134,10 @@
     value_gradient = value_gradient_sum.reshape(rows_per_block, -1).astype(jnp.bfloat16)
     local_width = key_gradient.shape[-1]
     feature_cols = features.shape[-1]
-    piece = lax.all_gather(key_gradient[None], "fsdp", axis=0, tiled=True)
+    piece = jnp.concatenate(
+        lax.all_to_all(jnp.stack([key_gradient[None]] * lax.axis_size("fsdp")), "fsdp", 0, 0),
+        axis=0,
+    )
     count = piece.shape[0]
     indices = lax.iota(jnp.int32, count)
     seq_ids = indices // HEAD_GROUPS

time: 848 us -> 815 us (0.961)
  waiting for transfers between devices: 381 us -> 332 us
  starting transfers between devices: 396 us -> 413 us
    all_gather x1 -> x0, waiting for transfers between devices: 63.8 us -> none  [local(): piece = lax.all_gather(key_gradient[None], 'fsdp', axis=0, tiled=True)]
    all_to_all x0 -> x1, waiting for transfers between devices: none -> 23.1 us  [local(): lax.all_to_all(jnp.stack([key_gradient[None]] * lax.axis_size('fsdp')), '...]
    all_to_all x0 -> x1, starting transfers between devices: none -> 14.2 us  [local(): lax.all_to_all(jnp.stack([key_gradient[None]] * lax.axis_size('fsdp')), '...]
where the time goes in v1:
time: 815 us; the launch traced here: 812 us
  starting transfers between devices  413 us (51%)
  waiting for transfers between devices  332 us (41%)
  matrix products  18.4 us (2%)
  between operations  14.8 us (2%)
  other arithmetic  12.4 us (2%)
  local copies, waits for them, and re-layouts  11.3 us (1%)
  loops' own time  10 us (1%)
    ppermute x77, starting transfers between devices, from_behind(): return lax.ppermute(value, axis, pairs)  399 us
    psum x1, waiting for transfers between devices, local(): grad_wk = lax.psum(summed, 'ctx')  194 us
    ppermute x77, waiting for transfers between devices, from_behind(): return lax.ppermute(value, axis, pairs)  115 us
    all_to_all x1, waiting for transfers between devices, local(): lax.all_to_all(jnp.stack([key_gradient[None]] * lax.axis_size('fsdp')), '...  23.1 us
  transfers between devices with their start and end apart: 79, of which 30 were waited for; matrix products, arithmetic and copies ran while one was open for 4% of the time, Pallas kernels for 0%

profile of v1, /device:TPU:2, one launch (start us, length us, event | category | flops | bytes accessed | tf_op | source)
XLA Modules:
  0.0 812.0 jit_solution(7907084356041453456)
XLA Ops:
  12.6 538.8 %while.23 = (s32[]{:T(128)}, f32[128,1,5,128]{3,0,2,1:T(8,128)S(1)}, bf16[128,1,128]{2,0,1:T(8,128)(2,1)S(1)}, bf16[128,1,128]{2,0,1:T(8,128)(2,1)S(1)}, s32[1]{...) while((s32[]{:T(128)}, ...), condition=%wide.region_2.3_spmd.clone, body=%wide.region_1.2_spmd.clone.sunk | while | flops 105726208 | bytes 4103563 | solution.py:127
  12.6 9.1 %collective-permute-start = (bf16[128,1,128]{2,0,1:T(8,128)(2,1)S(1)}, bf16[128,1,128]{2,0,1:T(8,128)(2,1)S(1)}, u32[]{:S(2)}, u32[]{:S(2)}) collective-permute-start(bf16[128,1,128]{2,0,1:T(8,128)(2,1)S(1)} %copy.66), channel_id=1, source_target_pairs={{0,32},{32,64},{64,96},{96,128},{128,160},{160,192},{192,224},{224... | collective-permute-start | bytes 98312 | tf_op jit(solution)/shard_map/while/body/eval_jaxpr/ppermute | solution.py:15
  21.7 9.1 %collective-permute-start.1 = (bf16[128,1,128]{2,0,1:T(8,128)(2,1)S(1)}, bf16[128,1,128]{2,0,1:T(8,128)(2,1)S(1)}, u32[]{:S(2)}, u32[]{:S(2)}) collective-permute-start(bf16[128,1,128]{2,0,1:T(8,128)(2,1)S(1)} %copy.67), channel_id=1, source_target_pairs={{0,32},{32,64},{64,96},{96,128},{128,160},{160,192},{192,224},{224... | collective-permute-start | bytes 98312 | tf_op jit(solution)/shard_map/while/body/eval_jaxpr/ppermute | solution.py:15
  31.3 5.6 collective-permute-start.2
  45.9 7.4 collective-permute-done.3
  57.8 8.3 %collective-permute-start.1 = (bf16[128,1,128]{2,0,1:T(8,128)(2,1)S(1)}, bf16[128,1,128]{2,0,1:T(8,128)(2,1)S(1)}, u32[]{:S(2)}, u32[]{:S(2)}) collective-permute-start(bf16[128,1,128]{2,0,1:T(8,128)(2,1)S(1)} %copy.67), channel_id=1, source_target_pairs={{0,32},{32,64},{64,96},{96,128},{128,160},{160,192},{192,224},{224... | collective-permute-start | bytes 98312 | tf_op jit(solution)/shard_map/while/body/eval_jaxpr/ppermute | solution.py:15
  84.2 5.4 collective-permute-done.4
  94.6 8.3 %collective-permute-start.1 = (bf16[128,1,128]{2,0,1:T(8,128)(2,1)S(1)}, bf16[128,1,128]{2,0,1:T(8,128)(2,1)S(1)}, u32[]{:S(2)}, u32[]{:S(2)}) collective-permute-start(bf16[128,1,128]{2,0,1:T(8,128)(2,1)S(1)} %copy.67), channel_id=1, source_target_pairs={{0,32},{32,64},{64,96},{96,128},{128,160},{160,192},{192,224},{224... | collective-permute-start | bytes 98312 | tf_op jit(solution)/shard_map/while/body/eval_jaxpr/ppermute | solution.py:15
  124.1 7.5 collective-permute-start
  131.6 6.5 collective-permute-start.1
  148.4 6.7 collective-permute-start.4
  159.7 6.4 collective-permute-start
  166.1 5.5 collective-permute-start.1
  177.0 6.6 collective-permute-start.3
  183.8 6.8 collective-permute-start.4
  195.1 5.7 collective-permute-start
  200.8 6.4 collective-permute-start.1
  207.8 5.7 collective-permute-start.2
  215.0 5.4 collective-permute-start.3
  220.6 8.3 %collective-permute-start.4 = (f32[128,1,128]{2,0,1:T(8,128)S(1)}, f32[128,1,128]{2,0,1:T(8,128)S(1)}, u32[]{:S(2)}, u32[]{:S(2)}) collective-permute-start(f32[128,1,128]{2,0,1:T(8,128)S(1)} %fusion.90), channel_id=1, source_target_pairs={{0,32},{32,64},{64,96},{96,128},{128,160},{160,192},{192,224},{224... | collective-permute-start | bytes 196616 | tf_op jit(solution)/shard_map/while/body/eval_jaxpr/ppermute | solution.py:15
  232.8 7.4 collective-permute-start
  268.0 7.3 collective-permute-start.1
  275.9 8.1 collective-permute-start.2
  285.4 5.7 collective-permute-start.3
  296.7 6.8 collective-permute-done.4
  309.5 9.6 %collective-permute-start.2 = (s32[1]{0:T(128)}, s32[1]{0:T(128)}, u32[]{:S(2)}, u32[]{:S(2)}) collective-permute-start(s32[1]{0:T(128)} %copy.68), channel_id=1, source_target_pairs={{0,32},{32,64},{64,96},{96,128},{128,160},{160,192},{192,224},{224... | collective-permute-start | bytes 20 | tf_op jit(solution)/shard_map/while/body/eval_jaxpr/ppermute | solution.py:15
  320.5 5.5 collective-permute-start.3
  333.6 5.9 collective-permute-done.4
  344.0 8.7 %collective-permute-start.2 = (s32[1]{0:T(128)}, s32[1]{0:T(128)}, u32[]{:S(2)}, u32[]{:S(2)}) collective-permute-start(s32[1]{0:T(128)} %copy.68), channel_id=1, source_target_pairs={{0,32},{32,64},{64,96},{96,128},{128,160},{160,192},{192,224},{224... | collective-permute-start | bytes 20 | tf_op jit(solution)/shard_map/while/body/eval_jaxpr/ppermute | solution.py:15
  354.0 9.3 %collective-permute-start.3 = (f32[128,1,128]{2,0,1:T(8,128)S(1)}, f32[128,1,128]{2,0,1:T(8,128)S(1)}, u32[]{:S(2)}, u32[]{:S(2)}) collective-permute-start(f32[128,1,128]{2,0,1:T(8,128)S(1)} %fusion.89), channel_id=1, source_target_pairs={{0,32},{32,64},{64,96},{96,128},{128,160},{160,192},{192,224},{224... | collective-permute-start | bytes 196616 | tf_op jit(solution)/shard_map/while/body/eval_jaxpr/ppermute | solution.py:15
  363.6 8.3 %collective-permute-start.4 = (f32[128,1,128]{2,0,1:T(8,128)S(1)}, f32[128,1,128]{2,0,1:T(8,128)S(1)}, u32[]{:S(2)}, u32[]{:S(2)}) collective-permute-start(f32[128,1,128]{2,0,1:T(8,128)S(1)} %fusion.90), channel_id=1, source_target_pairs={{0,32},{32,64},{64,96},{96,128},{128,160},{160,192},{192,224},{224... | collective-permute-start | bytes 196616 | tf_op jit(solution)/shard_map/while/body/eval_jaxpr/ppermute | solution.py:15
  376.5 8.3 %collective-permute-start = (bf16[128,1,128]{2,0,1:T(8,128)(2,1)S(1)}, bf16[128,1,128]{2,0,1:T(8,128)(2,1)S(1)}, u32[]{:S(2)}, u32[]{:S(2)}) collective-permute-start(bf16[128,1,128]{2,0,1:T(8,128)(2,1)S(1)} %copy.66), channel_id=1, source_target_pairs={{0,32},{32,64},{64,96},{96,128},{128,160},{160,192},{192,224},{224... | collective-permute-start | bytes 98312 | tf_op jit(solution)/shard_map/while/body/eval_jaxpr/ppermute | solution.py:15
  398.8 5.4 collective-permute-done.3
  414.8 10.6 %collective-permute-start.2 = (s32[1]{0:T(128)}, s32[1]{0:T(128)}, u32[]{:S(2)}, u32[]{:S(2)}) collective-permute-start(s32[1]{0:T(128)} %copy.68), channel_id=1, source_target_pairs={{0,32},{32,64},{64,96},{96,128},{128,160},{160,192},{192,224},{224... | collective-permute-start | bytes 20 | tf_op jit(solution)/shard_map/while/body/eval_jaxpr/ppermute | solution.py:15
  426.8 7.3 collective-permute-start.3
  438.1 7.5 collective-permute-done.4
  448.8 6.1 collective-permute-start.1
  455.4 9.9 %collective-permute-start.2 = (s32[1]{0:T(128)}, s32[1]{0:T(128)}, u32[]{:S(2)}, u32[]{:S(2)}) collective-permute-start(s32[1]{0:T(128)} %copy.68), channel_id=1, source_target_pairs={{0,32},{32,64},{64,96},{96,128},{128,160},{160,192},{192,224},{224... | collective-permute-start | bytes 20 | tf_op jit(solution)/shard_map/while/body/eval_jaxpr/ppermute | solution.py:15
  466.7 6.3 collective-permute-start.3
  478.7 7.5 collective-permute-done.4
  490.5 6.8 collective-permute-start.2
  498.8 11.2 %collective-permute-start.3 = (f32[128,1,128]{2,0,1:T(8,128)S(1)}, f32[128,1,128]{2,0,1:T(8,128)S(1)}, u32[]{:S(2)}, u32[]{:S(2)}) collective-permute-start(f32[128,1,128]{2,0,1:T(8,128)S(1)} %fusion.89), channel_id=1, source_target_pairs={{0,32},{32,64},{64,96},{96,128},{128,160},{160,192},{192,224},{224... | collective-permute-start | bytes 196616 | tf_op jit(solution)/shard_map/while/body/eval_jaxpr/ppermute | solution.py:15
  510.2 8.9 %collective-permute-start.4 = (f32[128,1,128]{2,0,1:T(8,128)S(1)}, f32[128,1,128]{2,0,1:T(8,128)S(1)}, u32[]{:S(2)}, u32[]{:S(2)}) collective-permute-start(f32[128,1,128]{2,0,1:T(8,128)S(1)} %fusion.90), channel_id=1, source_target_pairs={{0,32},{32,64},{64,96},{96,128},{128,160},{160,192},{192,224},{224... | collective-permute-start | bytes 196616 | tf_op jit(solution)/shard_map/while/body/eval_jaxpr/ppermute | solution.py:15
  522.0 8.4 %collective-permute-start = (bf16[128,1,128]{2,0,1:T(8,128)(2,1)S(1)}, bf16[128,1,128]{2,0,1:T(8,128)(2,1)S(1)}, u32[]{:S(2)}, u32[]{:S(2)}) collective-permute-start(bf16[128,1,128]{2,0,1:T(8,128)(2,1)S(1)} %copy.66), channel_id=1, source_target_pairs={{0,32},{32,64},{64,96},{96,128},{128,160},{160,192},{192,224},{224... | collective-permute-start | bytes 98312 | tf_op jit(solution)/shard_map/while/body/eval_jaxpr/ppermute | solution.py:15
  555.3 8.7 %collective-permute-done.5 = bf16[128,1,128]{2,0,1:T(8,128)(2,1)S(1)} collective-permute-done((bf16[128,1,128]{2,0,1:T(8,128)(2,1)S(1)}, bf16[128,1,128]{2,0,1:T(8,128)(2,1)S(1)}, u32[]{:S(2)}, u32[]{:S(2)}) %collective-permute-start.5) | collective-permute-done | bytes 32800 | tf_op jit(solution)/shard_map/ppermute | solution.py:15
  565.2 14.2 %all-to-all-start = ((bf16[32,1,128,128]{3,2,1,0:T(8,128)(2,1)}), bf16[32,1,128,128]{3,2,1,0:T(8,128)(2,1)S(1)}, u32[]{:S(2)}, u32[]{:S(2)}) async-start(bf16[32,1,128,128]{3,2,1,0:T(8,128)(2,1)} %stack.3), calls=%async_computation | async-start | bytes 2097152 | tf_op jit(solution)/shard_map/all_to_all | solution.py:138
  582.5 23.1 %all-to-all-done = bf16[32,1,128,128]{3,2,1,0:T(8,128)(2,1)S(1)} async-done(((bf16[32,1,128,128]{3,2,1,0:T(8,128)(2,1)}), bf16[32,1,128,128]{3,2,1,0:T(8,128)(2,1)S(1)}, u32[]{:S(2)}, u32[]{:S(2)}) %all-to-all-start) | async-done | bytes 1048608 | tf_op jit(solution)/shard_map/all_to_all | solution.py:138
  608.3 194.1 %all-reduce.2.cloned.1.call-done = f32[80,512]{1,0:T(8,128)} async-done(((f32[80,512]{1,0:T(8,128)}), f32[80,512]{1,0:T(8,128)}) %all-reduce.2.cloned.1.call-update) | async-done | bytes 163856 | tf_op jit(solution)/shard_map/psum | solution.py:151
  (311 shorter events, 229.9 us)
Async XLA Ops:
  12.6 33.3 %collective-permute-start = (bf16[128,1,128]{2,0,1:T(8,128)(2,1)S(1)}, bf16[128,1,128]{2,0,1:T(8,128)(2,1)S(1)}, u32[]{:S(2)}, u32[]{:S(2)}) collective-permute-start(bf16[128,1,128]{2,0,1:T(8,128)(2,1)S(1)} %copy.66), channel_id=1, source_target_pairs={{0,32},{32,64},{64,96},{96,128},{128,160},{160,192},{192,224},{224... | collective-permute-start | bytes 98312 | tf_op jit(solution)/shard_map/while/body/eval_jaxpr/ppermute | solution.py:15
  21.7 24.2 %collective-permute-start.1 = (bf16[128,1,128]{2,0,1:T(8,128)(2,1)S(1)}, bf16[128,1,128]{2,0,1:T(8,128)(2,1)S(1)}, u32[]{:S(2)}, u32[]{:S(2)}) collective-permute-start(bf16[128,1,128]{2,0,1:T(8,128)(2,1)S(1)} %copy.67), channel_id=1, source_target_pairs={{0,32},{32,64},{64,96},{96,128},{128,160},{160,192},{192,224},{224... | collective-permute-start | bytes 98312 | tf_op jit(solution)/shard_map/while/body/eval_jaxpr/ppermute | solution.py:15
  31.3 14.5 %collective-permute-start.2 = (s32[1]{0:T(128)}, s32[1]{0:T(128)}, u32[]{:S(2)}, u32[]{:S(2)}) collective-permute-start(s32[1]{0:T(128)} %copy.68), channel_id=1, source_target_pairs={{0,32},{32,64},{64,96},{96,128},{128,160},{160,192},{192,224},{224... | collective-permute-start | bytes 20 | tf_op jit(solution)/shard_map/while/body/eval_jaxpr/ppermute | solution.py:15
  38.3 14.9 %collective-permute-start.3 = (f32[128,1,128]{2,0,1:T(8,128)S(1)}, f32[128,1,128]{2,0,1:T(8,128)S(1)}, u32[]{:S(2)}, u32[]{:S(2)}) collective-permute-start(f32[128,1,128]{2,0,1:T(8,128)S(1)} %fusion.89), channel_id=1, source_target_pairs={{0,32},{32,64},{64,96},{96,128},{128,160},{160,192},{192,224},{224... | collective-permute-start | bytes 196616 | tf_op jit(solution)/shard_map/while/body/eval_jaxpr/ppermute | solution.py:15
  54.0 27.8 %collective-permute-start = (bf16[128,1,128]{2,0,1:T(8,128)(2,1)S(1)}, bf16[128,1,128]{2,0,1:T(8,128)(2,1)S(1)}, u32[]{:S(2)}, u32[]{:S(2)}) collective-permute-start(bf16[128,1,128]{2,0,1:T(8,128)(2,1)S(1)} %copy.66), channel_id=1, source_target_pairs={{0,32},{32,64},{64,96},{96,128},{128,160},{160,192},{192,224},{224... | collective-permute-start | bytes 98312 | tf_op jit(solution)/shard_map/while/body/eval_jaxpr/ppermute | solution.py:15
  57.8 24.0 %collective-permute-start.1 = (bf16[128,1,128]{2,0,1:T(8,128)(2,1)S(1)}, bf16[128,1,128]{2,0,1:T(8,128)(2,1)S(1)}, u32[]{:S(2)}, u32[]{:S(2)}) collective-permute-start(bf16[128,1,128]{2,0,1:T(8,128)(2,1)S(1)} %copy.67), channel_id=1, source_target_pairs={{0,32},{32,64},{64,96},{96,128},{128,160},{160,192},{192,224},{224... | collective-permute-start | bytes 98312 | tf_op jit(solution)/shard_map/while/body/eval_jaxpr/ppermute | solution.py:15
  66.7 15.1 %collective-permute-start.2 = (s32[1]{0:T(128)}, s32[1]{0:T(128)}, u32[]{:S(2)}, u32[]{:S(2)}) collective-permute-start(s32[1]{0:T(128)} %copy.68), channel_id=1, source_target_pairs={{0,32},{32,64},{64,96},{96,128},{128,160},{160,192},{192,224},{224... | collective-permute-start | bytes 20 | tf_op jit(solution)/shard_map/while/body/eval_jaxpr/ppermute | solution.py:15
  89.6 28.8 %collective-permute-start = (bf16[128,1,128]{2,0,1:T(8,128)(2,1)S(1)}, bf16[128,1,128]{2,0,1:T(8,128)(2,1)S(1)}, u32[]{:S(2)}, u32[]{:S(2)}) collective-permute-start(bf16[128,1,128]{2,0,1:T(8,128)(2,1)S(1)} %copy.66), channel_id=1, source_target_pairs={{0,32},{32,64},{64,96},{96,128},{128,160},{160,192},{192,224},{224... | collective-permute-start | bytes 98312 | tf_op jit(solution)/shard_map/while/body/eval_jaxpr/ppermute | solution.py:15
  94.6 23.9 %collective-permute-start.1 = (bf16[128,1,128]{2,0,1:T(8,128)(2,1)S(1)}, bf16[128,1,128]{2,0,1:T(8,128)(2,1)S(1)}, u32[]{:S(2)}, u32[]{:S(2)}) collective-permute-start(bf16[128,1,128]{2,0,1:T(8,128)(2,1)S(1)} %copy.67), channel_id=1, source_target_pairs={{0,32},{32,64},{64,96},{96,128},{128,160},{160,192},{192,224},{224... | collective-permute-start | bytes 98312 | tf_op jit(solution)/shard_map/while/body/eval_jaxpr/ppermute | solution.py:15
  103.4 15.0 %collective-permute-start.2 = (s32[1]{0:T(128)}, s32[1]{0:T(128)}, u32[]{:S(2)}, u32[]{:S(2)}) collective-permute-start(s32[1]{0:T(128)} %copy.68), channel_id=1, source_target_pairs={{0,32},{32,64},{64,96},{96,128},{128,160},{160,192},{192,224},{224... | collective-permute-start | bytes 20 | tf_op jit(solution)/shard_map/while/body/eval_jaxpr/ppermute | solution.py:15
  124.1 31.4 %collective-permute-start = (bf16[128,1,128]{2,0,1:T(8,128)(2,1)S(1)}, bf16[128,1,128]{2,0,1:T(8,128)(2,1)S(1)}, u32[]{:S(2)}, u32[]{:S(2)}) collective-permute-start(bf16[128,1,128]{2,0,1:T(8,128)(2,1)S(1)} %copy.66), channel_id=1, source_target_pairs={{0,32},{32,64},{64,96},{96,128},{128,160},{160,192},{192,224},{224... | collective-permute-start | bytes 98312 | tf_op jit(solution)/shard_map/while/body/eval_jaxpr/ppermute | solution.py:15
  131.6 23.9 %collective-permute-start.1 = (bf16[128,1,128]{2,0,1:T(8,128)(2,1)S(1)}, bf16[128,1,128]{2,0,1:T(8,128)(2,1)S(1)}, u32[]{:S(2)}, u32[]{:S(2)}) collective-permute-start(bf16[128,1,128]{2,0,1:T(8,128)(2,1)S(1)} %copy.67), channel_id=1, source_target_pairs={{0,32},{32,64},{64,96},{96,128},{128,160},{160,192},{192,224},{224... | collective-permute-start | bytes 98312 | tf_op jit(solution)/shard_map/while/body/eval_jaxpr/ppermute | solution.py:15
  138.7 16.8 %collective-permute-start.2 = (s32[1]{0:T(128)}, s32[1]{0:T(128)}, u32[]{:S(2)}, u32[]{:S(2)}) collective-permute-start(s32[1]{0:T(128)} %copy.68), channel_id=1, source_target_pairs={{0,32},{32,64},{64,96},{96,128},{128,160},{160,192},{192,224},{224... | collective-permute-start | bytes 20 | tf_op jit(solution)/shard_map/while/body/eval_jaxpr/ppermute | solution.py:15
  159.7 31.2 %collective-permute-start = (bf16[128,1,128]{2,0,1:T(8,128)(2,1)S(1)}, bf16[128,1,128]{2,0,1:T(8,128)(2,1)S(1)}, u32[]{:S(2)}, u32[]{:S(2)}) collective-permute-start(bf16[128,1,128]{2,0,1:T(8,128)(2,1)S(1)} %copy.66), channel_id=1, source_target_pairs={{0,32},{32,64},{64,96},{96,128},{128,160},{160,192},{192,224},{224... | collective-permute-start | bytes 98312 | tf_op jit(solution)/shard_map/while/body/eval_jaxpr/ppermute | solution.py:15
  166.1 24.8 %collective-permute-start.1 = (bf16[128,1,128]{2,0,1:T(8,128)(2,1)S(1)}, bf16[128,1,128]{2,0,1:T(8,128)(2,1)S(1)}, u32[]{:S(2)}, u32[]{:S(2)}) collective-permute-start(bf16[128,1,128]{2,0,1:T(8,128)(2,1)S(1)} %copy.67), channel_id=1, source_target_pairs={{0,32},{32,64},{64,96},{96,128},{128,160},{160,192},{192,224},{224... | collective-permute-start | bytes 98312 | tf_op jit(solution)/shard_map/while/body/eval_jaxpr/ppermute | solution.py:15
  172.2 18.7 %collective-permute-start.2 = (s32[1]{0:T(128)}, s32[1]{0:T(128)}, u32[]{:S(2)}, u32[]{:S(2)}) collective-permute-start(s32[1]{0:T(128)} %copy.68), channel_id=1, source_target_pairs={{0,32},{32,64},{64,96},{96,128},{128,160},{160,192},{192,224},{224... | collective-permute-start | bytes 20 | tf_op jit(solution)/shard_map/while/body/eval_jaxpr/ppermute | solution.py:15
  195.1 34.0 %collective-permute-start = (bf16[128,1,128]{2,0,1:T(8,128)(2,1)S(1)}, bf16[128,1,128]{2,0,1:T(8,128)(2,1)S(1)}, u32[]{:S(2)}, u32[]{:S(2)}) collective-permute-start(bf16[128,1,128]{2,0,1:T(8,128)(2,1)S(1)} %copy.66), channel_id=1, source_target_pairs={{0,32},{32,64},{64,96},{96,128},{128,160},{160,192},{192,224},{224... | collective-permute-start | bytes 98312 | tf_op jit(solution)/shard_map/while/body/eval_jaxpr/ppermute | solution.py:15
  200.8 28.3 %collective-permute-start.1 = (bf16[128,1,128]{2,0,1:T(8,128)(2,1)S(1)}, bf16[128,1,128]{2,0,1:T(8,128)(2,1)S(1)}, u32[]{:S(2)}, u32[]{:S(2)}) collective-permute-start(bf16[128,1,128]{2,0,1:T(8,128)(2,1)S(1)} %copy.67), channel_id=1, source_target_pairs={{0,32},{32,64},{64,96},{96,128},{128,160},{160,192},{192,224},{224... | collective-permute-start | bytes 98312 | tf_op jit(solution)/shard_map/while/body/eval_jaxpr/ppermute | solution.py:15
  207.8 21.3 %collective-permute-start.2 = (s32[1]{0:T(128)}, s32[1]{0:T(128)}, u32[]{:S(2)}, u32[]{:S(2)}) collective-permute-start(s32[1]{0:T(128)} %copy.68), channel_id=1, source_target_pairs={{0,32},{32,64},{64,96},{96,128},{128,160},{160,192},{192,224},{224... | collective-permute-start | bytes 20 | tf_op jit(solution)/shard_map/while/body/eval_jaxpr/ppermute | solution.py:15
  215.0 14.2 %collective-permute-start.3 = (f32[128,1,128]{2,0,1:T(8,128)S(1)}, f32[128,1,128]{2,0,1:T(8,128)S(1)}, u32[]{:S(2)}, u32[]{:S(2)}) collective-permute-start(f32[128,1,128]{2,0,1:T(8,128)S(1)} %fusion.89), channel_id=1, source_target_pairs={{0,32},{32,64},{64,96},{96,128},{128,160},{160,192},{192,224},{224... | collective-permute-start | bytes 196616 | tf_op jit(solution)/shard_map/while/body/eval_jaxpr/ppermute | solution.py:15
  232.8 24.8 %collective-permute-start = (bf16[128,1,128]{2,0,1:T(8,128)(2,1)S(1)}, bf16[128,1,128]{2,0,1:T(8,128)(2,1)S(1)}, u32[]{:S(2)}, u32[]{:S(2)}) collective-permute-start(bf16[128,1,128]{2,0,1:T(8,128)(2,1)S(1)} %copy.66), channel_id=1, source_target_pairs={{0,32},{32,64},{64,96},{96,128},{128,160},{160,192},{192,224},{224... | collective-permute-start | bytes 98312 | tf_op jit(solution)/shard_map/while/body/eval_jaxpr/ppermute | solution.py:15
  240.3 17.3 %collective-permute-start.1 = (bf16[128,1,128]{2,0,1:T(8,128)(2,1)S(1)}, bf16[128,1,128]{2,0,1:T(8,128)(2,1)S(1)}, u32[]{:S(2)}, u32[]{:S(2)}) collective-permute-start(bf16[128,1,128]{2,0,1:T(8,128)(2,1)S(1)} %copy.67), channel_id=1, source_target_pairs={{0,32},{32,64},{64,96},{96,128},{128,160},{160,192},{192,224},{224... | collective-permute-start | bytes 98312 | tf_op jit(solution)/shard_map/while/body/eval_jaxpr/ppermute | solution.py:15
  264.7 29.0 %collective-permute-start = (bf16[128,1,128]{2,0,1:T(8,128)(2,1)S(1)}, bf16[128,1,128]{2,0,1:T(8,128)(2,1)S(1)}, u32[]{:S(2)}, u32[]{:S(2)}) collective-permute-start(bf16[128,1,128]{2,0,1:T(8,128)(2,1)S(1)} %copy.66), channel_id=1, source_target_pairs={{0,32},{32,64},{64,96},{96,128},{128,160},{160,192},{192,224},{224... | collective-permute-start | bytes 98312 | tf_op jit(solution)/shard_map/while/body/eval_jaxpr/ppermute | solution.py:15
  268.0 25.7 %collective-permute-start.1 = (bf16[128,1,128]{2,0,1:T(8,128)(2,1)S(1)}, bf16[128,1,128]{2,0,1:T(8,128)(2,1)S(1)}, u32[]{:S(2)}, u32[]{:S(2)}) collective-permute-start(bf16[128,1,128]{2,0,1:T(8,128)(2,1)S(1)} %copy.67), channel_id=1, source_target_pairs={{0,32},{32,64},{64,96},{96,128},{128,160},{160,192},{192,224},{224... | collective-permute-start | bytes 98312 | tf_op jit(solution)/shard_map/while/body/eval_jaxpr/ppermute | solution.py:15
  275.9 17.8 %collective-permute-start.2 = (s32[1]{0:T(128)}, s32[1]{0:T(128)}, u32[]{:S(2)}, u32[]{:S(2)}) collective-permute-start(s32[1]{0:T(128)} %copy.68), channel_id=1, source_target_pairs={{0,32},{32,64},{64,96},{96,128},{128,160},{160,192},{192,224},{224... | collective-permute-start | bytes 20 | tf_op jit(solution)/shard_map/while/body/eval_jaxpr/ppermute | solution.py:15
  303.4 25.0 %collective-permute-start = (bf16[128,1,128]{2,0,1:T(8,128)(2,1)S(1)}, bf16[128,1,128]{2,0,1:T(8,128)(2,1)S(1)}, u32[]{:S(2)}, u32[]{:S(2)}) collective-permute-start(bf16[128,1,128]{2,0,1:T(8,128)(2,1)S(1)} %copy.66), channel_id=1, source_target_pairs={{0,32},{32,64},{64,96},{96,128},{128,160},{160,192},{192,224},{224... | collective-permute-start | bytes 98312 | tf_op jit(solution)/shard_map/while/body/eval_jaxpr/ppermute | solution.py:15
  305.4 23.1 %collective-permute-start.1 = (bf16[128,1,128]{2,0,1:T(8,128)(2,1)S(1)}, bf16[128,1,128]{2,0,1:T(8,128)(2,1)S(1)}, u32[]{:S(2)}, u32[]{:S(2)}) collective-permute-start(bf16[128,1,128]{2,0,1:T(8,128)(2,1)S(1)} %copy.67), channel_id=1, source_target_pairs={{0,32},{32,64},{64,96},{96,128},{128,160},{160,192},{192,224},{224... | collective-permute-start | bytes 98312 | tf_op jit(solution)/shard_map/while/body/eval_jaxpr/ppermute | solution.py:15
  309.5 18.9 %collective-permute-start.2 = (s32[1]{0:T(128)}, s32[1]{0:T(128)}, u32[]{:S(2)}, u32[]{:S(2)}) collective-permute-start(s32[1]{0:T(128)} %copy.68), channel_id=1, source_target_pairs={{0,32},{32,64},{64,96},{96,128},{128,160},{160,192},{192,224},{224... | collective-permute-start | bytes 20 | tf_op jit(solution)/shard_map/while/body/eval_jaxpr/ppermute | solution.py:15
  339.5 32.7 %collective-permute-start = (bf16[128,1,128]{2,0,1:T(8,128)(2,1)S(1)}, bf16[128,1,128]{2,0,1:T(8,128)(2,1)S(1)}, u32[]{:S(2)}, u32[]{:S(2)}) collective-permute-start(bf16[128,1,128]{2,0,1:T(8,128)(2,1)S(1)} %copy.66), channel_id=1, source_target_pairs={{0,32},{32,64},{64,96},{96,128},{128,160},{160,192},{192,224},{224... | collective-permute-start | bytes 98312 | tf_op jit(solution)/shard_map/while/body/eval_jaxpr/ppermute | solution.py:15
  341.4 30.7 %collective-permute-start.1 = (bf16[128,1,128]{2,0,1:T(8,128)(2,1)S(1)}, bf16[128,1,128]{2,0,1:T(8,128)(2,1)S(1)}, u32[]{:S(2)}, u32[]{:S(2)}) collective-permute-start(bf16[128,1,128]{2,0,1:T(8,128)(2,1)S(1)} %copy.67), channel_id=1, source_target_pairs={{0,32},{32,64},{64,96},{96,128},{128,160},{160,192},{192,224},{224... | collective-permute-start | bytes 98312 | tf_op jit(solution)/shard_map/while/body/eval_jaxpr/ppermute | solution.py:15
  344.0 28.1 %collective-permute-start.2 = (s32[1]{0:T(128)}, s32[1]{0:T(128)}, u32[]{:S(2)}, u32[]{:S(2)}) collective-permute-start(s32[1]{0:T(128)} %copy.68), channel_id=1, source_target_pairs={{0,32},{32,64},{64,96},{96,128},{128,160},{160,192},{192,224},{224... | collective-permute-start | bytes 20 | tf_op jit(solution)/shard_map/while/body/eval_jaxpr/ppermute | solution.py:15
  354.0 18.1 %collective-permute-start.3 = (f32[128,1,128]{2,0,1:T(8,128)S(1)}, f32[128,1,128]{2,0,1:T(8,128)S(1)}, u32[]{:S(2)}, u32[]{:S(2)}) collective-permute-start(f32[128,1,128]{2,0,1:T(8,128)S(1)} %fusion.89), channel_id=1, source_target_pairs={{0,32},{32,64},{64,96},{96,128},{128,160},{160,192},{192,224},{224... | collective-permute-start | bytes 196616 | tf_op jit(solution)/shard_map/while/body/eval_jaxpr/ppermute | solution.py:15
  376.5 22.3 %collective-permute-start = (bf16[128,1,128]{2,0,1:T(8,128)(2,1)S(1)}, bf16[128,1,128]{2,0,1:T(8,128)(2,1)S(1)}, u32[]{:S(2)}, u32[]{:S(2)}) collective-permute-start(bf16[128,1,128]{2,0,1:T(8,128)(2,1)S(1)} %copy.66), channel_id=1, source_target_pairs={{0,32},{32,64},{64,96},{96,128},{128,160},{160,192},{192,224},{224... | collective-permute-start | bytes 98312 | tf_op jit(solution)/shard_map/while/body/eval_jaxpr/ppermute | solution.py:15
  384.8 14.0 %collective-permute-start.1 = (bf16[128,1,128]{2,0,1:T(8,128)(2,1)S(1)}, bf16[128,1,128]{2,0,1:T(8,128)(2,1)S(1)}, u32[]{:S(2)}, u32[]{:S(2)}) collective-permute-start(bf16[128,1,128]{2,0,1:T(8,128)(2,1)S(1)} %copy.67), channel_id=1, source_target_pairs={{0,32},{32,64},{64,96},{96,128},{128,160},{160,192},{192,224},{224... | collective-permute-start | bytes 98312 | tf_op jit(solution)/shard_map/while/body/eval_jaxpr/ppermute | solution.py:15
  407.8 28.9 %collective-permute-start = (bf16[128,1,128]{2,0,1:T(8,128)(2,1)S(1)}, bf16[128,1,128]{2,0,1:T(8,128)(2,1)S(1)}, u32[]{:S(2)}, u32[]{:S(2)}) collective-permute-start(bf16[128,1,128]{2,0,1:T(8,128)(2,1)S(1)} %copy.66), channel_id=1, source_target_pairs={{0,32},{32,64},{64,96},{96,128},{128,160},{160,192},{192,224},{224... | collective-permute-start | bytes 98312 | tf_op jit(solution)/shard_map/while/body/eval_jaxpr/ppermute | solution.py:15
  409.7 26.9 %collective-permute-start.1 = (bf16[128,1,128]{2,0,1:T(8,128)(2,1)S(1)}, bf16[128,1,128]{2,0,1:T(8,128)(2,1)S(1)}, u32[]{:S(2)}, u32[]{:S(2)}) collective-permute-start(bf16[128,1,128]{2,0,1:T(8,128)(2,1)S(1)} %copy.67), channel_id=1, source_target_pairs={{0,32},{32,64},{64,96},{96,128},{128,160},{160,192},{192,224},{224... | collective-permute-start | bytes 98312 | tf_op jit(solution)/shard_map/while/body/eval_jaxpr/ppermute | solution.py:15
  414.8 21.8 %collective-permute-start.2 = (s32[1]{0:T(128)}, s32[1]{0:T(128)}, u32[]{:S(2)}, u32[]{:S(2)}) collective-permute-start(s32[1]{0:T(128)} %copy.68), channel_id=1, source_target_pairs={{0,32},{32,64},{64,96},{96,128},{128,160},{160,192},{192,224},{224... | collective-permute-start | bytes 20 | tf_op jit(solution)/shard_map/while/body/eval_jaxpr/ppermute | solution.py:15
  445.6 29.9 %collective-permute-start = (bf16[128,1,128]{2,0,1:T(8,128)(2,1)S(1)}, bf16[128,1,128]{2,0,1:T(8,128)(2,1)S(1)}, u32[]{:S(2)}, u32[]{:S(2)}) collective-permute-start(bf16[128,1,128]{2,0,1:T(8,128)(2,1)S(1)} %copy.66), channel_id=1, source_target_pairs={{0,32},{32,64},{64,96},{96,128},{128,160},{160,192},{192,224},{224... | collective-permute-start | bytes 98312 | tf_op jit(solution)/shard_map/while/body/eval_jaxpr/ppermute | solution.py:15
  448.8 26.7 %collective-permute-start.1 = (bf16[128,1,128]{2,0,1:T(8,128)(2,1)S(1)}, bf16[128,1,128]{2,0,1:T(8,128)(2,1)S(1)}, u32[]{:S(2)}, u32[]{:S(2)}) collective-permute-start(bf16[128,1,128]{2,0,1:T(8,128)(2,1)S(1)} %copy.67), channel_id=1, source_target_pairs={{0,32},{32,64},{64,96},{96,128},{128,160},{160,192},{192,224},{224... | collective-permute-start | bytes 98312 | tf_op jit(solution)/shard_map/while/body/eval_jaxpr/ppermute | solution.py:15
  455.4 20.0 %collective-permute-start.2 = (s32[1]{0:T(128)}, s32[1]{0:T(128)}, u32[]{:S(2)}, u32[]{:S(2)}) collective-permute-start(s32[1]{0:T(128)} %copy.68), channel_id=1, source_target_pairs={{0,32},{32,64},{64,96},{96,128},{128,160},{160,192},{192,224},{224... | collective-permute-start | bytes 20 | tf_op jit(solution)/shard_map/while/body/eval_jaxpr/ppermute | solution.py:15
  486.1 33.2 %collective-permute-start = (bf16[128,1,128]{2,0,1:T(8,128)(2,1)S(1)}, bf16[128,1,128]{2,0,1:T(8,128)(2,1)S(1)}, u32[]{:S(2)}, u32[]{:S(2)}) collective-permute-start(bf16[128,1,128]{2,0,1:T(8,128)(2,1)S(1)} %copy.66), channel_id=1, source_target_pairs={{0,32},{32,64},{64,96},{96,128},{128,160},{160,192},{192,224},{224... | collective-permute-start | bytes 98312 | tf_op jit(solution)/shard_map/while/body/eval_jaxpr/ppermute | solution.py:15
  488.1 31.3 %collective-permute-start.1 = (bf16[128,1,128]{2,0,1:T(8,128)(2,1)S(1)}, bf16[128,1,128]{2,0,1:T(8,128)(2,1)S(1)}, u32[]{:S(2)}, u32[]{:S(2)}) collective-permute-start(bf16[128,1,128]{2,0,1:T(8,128)(2,1)S(1)} %copy.67), channel_id=1, source_target_pairs={{0,32},{32,64},{64,96},{96,128},{128,160},{160,192},{192,224},{224... | collective-permute-start | bytes 98312 | tf_op jit(solution)/shard_map/while/body/eval_jaxpr/ppermute | solution.py:15
  490.5 28.8 %collective-permute-start.2 = (s32[1]{0:T(128)}, s32[1]{0:T(128)}, u32[]{:S(2)}, u32[]{:S(2)}) collective-permute-start(s32[1]{0:T(128)} %copy.68), channel_id=1, source_target_pairs={{0,32},{32,64},{64,96},{96,128},{128,160},{160,192},{192,224},{224... | collective-permute-start | bytes 20 | tf_op jit(solution)/shard_map/while/body/eval_jaxpr/ppermute | solution.py:15
  498.8 20.6 %collective-permute-start.3 = (f32[128,1,128]{2,0,1:T(8,128)S(1)}, f32[128,1,128]{2,0,1:T(8,128)S(1)}, u32[]{:S(2)}, u32[]{:S(2)}) collective-permute-start(f32[128,1,128]{2,0,1:T(8,128)S(1)} %fusion.89), channel_id=1, source_target_pairs={{0,32},{32,64},{64,96},{96,128},{128,160},{160,192},{192,224},{224... | collective-permute-start | bytes 196616 | tf_op jit(solution)/shard_map/while/body/eval_jaxpr/ppermute | solution.py:15
  522.0 22.0 %collective-permute-start = (bf16[128,1,128]{2,0,1:T(8,128)(2,1)S(1)}, bf16[128,1,128]{2,0,1:T(8,128)(2,1)S(1)}, u32[]{:S(2)}, u32[]{:S(2)}) collective-permute-start(bf16[128,1,128]{2,0,1:T(8,128)(2,1)S(1)} %copy.66), channel_id=1, source_target_pairs={{0,32},{32,64},{64,96},{96,128},{128,160},{160,192},{192,224},{224... | collective-permute-start | bytes 98312 | tf_op jit(solution)/shard_map/while/body/eval_jaxpr/ppermute | solution.py:15
  565.2 40.4 %all-to-all-start = ((bf16[32,1,128,128]{3,2,1,0:T(8,128)(2,1)}), bf16[32,1,128,128]{3,2,1,0:T(8,128)(2,1)S(1)}, u32[]{:S(2)}, u32[]{:S(2)}) async-start(bf16[32,1,128,128]{3,2,1,0:T(8,128)(2,1)} %stack.3), calls=%async_computation | async-start | bytes 2097152 | tf_op jit(solution)/shard_map/all_to_all | solution.py:138
  579.4 223.0 %all-reduce.2.cloned.1.call-start = ((), (), s32[]{:S(2)}) async-start(), calls=%async_computation.1 | async-start | bytes 327680 | tf_op jit(solution)/shard_map/psum | solution.py:151
  579.6 28.7 %collective-permute-start.6 = (bf16[128,1,128]{2,0,1:T(8,128)(2,1)S(1)}, bf16[128,1,128]{2,0,1:T(8,128)(2,1)S(1)}, u32[]{:S(2)}, u32[]{:S(2)}) collective-permute-start(bf16[128,1,128]{2,0,1:T(8,128)(2,1)S(1)} %fusion.33), channel_id=1, source_target_pairs={{0,32},{32,64},{64,96},{96,128},{128,160},{160,192},{192,224},{224... | collective-permute-start | bytes 98312 | tf_op jit(solution)/shard_map/ppermute | solution.py:15
  (39 other events, 953.0 us)
Sparse Core Ops, SparseCore 0:
  607.4 194.9 all-reduce.1
